TPU v7x, 32 devices: a whole 2x2x4 slice. The times are simulated.
32 devices in a mesh: grp: 4 (over x, core), ep: 8 (over z, y).
Axes of the slice: x: 2, y: 2, z: 4, core: 2. Of those that a mesh axis runs over, the one named last changes fastest.
Arguments:
- tokens: bfloat16 [32768, 512], P(('grp', 'ep')), may hold values from -6 to 6
- segments: int32 [128, 256], P(('grp', 'ep')), may hold values from 0 to 7, never falling along the last dimension, each value on 1 to 128 neighbouring positions
- patch_mask: int32 [128, 256], P(('grp', 'ep')), may hold values 0 or 1
- choices: int32 [32768, 2], P(('grp', 'ep')), may hold values from 0 to 7, all different within a row
- priority: int32 [32, 1024], P(('grp', 'ep')), may hold values from 0 to 1023, each once within a row
- first_gain: bfloat16 [512], P(('grp', 'ep')), may hold values from 0.5 to 1.5
- joint_weight: bfloat16 [512, 1536], P(('grp', 'ep')), may hold values from -0.25 to 0.25
- output_weight: bfloat16 [512, 512], P(('grp', 'ep')), may hold values from -1 to 1
- second_gain: bfloat16 [512], P(('grp', 'ep')), may hold values from 0.5 to 1.5
- router_weight: bfloat16 [512, 8], P(('grp', 'ep')), may hold values from -0.19921875 to 0.19921875
- expert_up: bfloat16 [8, 512, 2048], P('ep'), may hold values from -0.25 to 0.25
- expert_down: bfloat16 [8, 2048, 512], P('ep'), may hold values from -0.75 to 0.75
- out_grad: bfloat16 [32768, 512], P(('grp', 'ep')), may hold values from -6 to 6
Outputs:
- output: bfloat16 [32768, 512], P(('grp', 'ep'))
- tokens_grad: float32 [32768, 512], P(('grp', 'ep'))
- first_gain_grad: float32 [512], P(('grp', 'ep'))
- joint_weight_grad: float32 [512, 1536], P(('grp', 'ep'))
- output_weight_grad: float32 [512, 512], P(('grp', 'ep'))
- second_gain_grad: float32 [512], P(('grp', 'ep'))
- router_weight_grad: float32 [512, 8], P(('grp', 'ep'))
- expert_up_grad: float32 [8, 512, 2048], P('ep')
- expert_down_grad: float32 [8, 2048, 512], P('ep')
Inputs may be any that keep to these rules, and one draw needn't show every extreme that they name: `segments`: within a sequence the ids never fall. `choices`: a token's two experts differ. `priority`: each row holds every number below 1024 once.
All inputs are finite; a program needn't handle non-finite values. No bound on the sum of `patch_mask` on one device may be relied on, other than what follows from the above.
Results may differ from a plain program's by a relative error of at most 0.013.
Values may be sent and summed in bfloat16 or wider, within the bound.
A program may use at most 192 MiB of HBM per device.

v0:
```python
import jax
import jax.numpy as jnp
from jax import lax
from jax.sharding import PartitionSpec as P

HEADS = 8
EPSILON = 1e-06
NEGATIVE = -1e30


def normalize(values, gain):
    mean = jnp.mean(values, axis=-1, keepdims=True)
    centred = values - mean
    inverse = lax.rsqrt(jnp.mean(centred * centred, axis=-1, keepdims=True) + EPSILON)
    unit = centred * inverse
    return (unit * gain, unit, inverse)


def normalize_back(incoming, gain, unit, inverse):
    scaled = incoming * gain
    inner = (
        scaled
        - jnp.mean(scaled, axis=-1, keepdims=True)
        - unit * jnp.mean(scaled * unit, axis=-1, keepdims=True)
    )
    return (inverse * inner, jnp.sum(incoming * unit, axis=0))


def outer(left, right):
    return lax.dot_general(
        left, right, (((0,), (0,)), ((), ())), preferred_element_type=jnp.float32
    )


def times_t(left, right):
    return lax.dot_general(
        left, right, (((1,), (1,)), ((), ())), preferred_element_type=jnp.float32
    )


def gelu_slope(values):
    normal_cdf = 0.5 * (1.0 + lax.erf(values * 0.7071067811865476))
    density = jnp.exp(-0.5 * values * values) * 0.3989422804014327
    return normal_cdf + values * density


def route(picks, live, ranks, expert_count, capacity):
    row_count = picks.shape[0]
    labels = lax.broadcasted_iota(jnp.int32, (row_count, expert_count), 1)
    first = (picks[:, 0:1] == labels).astype(jnp.int32)
    second = (picks[:, 1:2] == labels).astype(jnp.int32)
    live_col = live[:, None]
    earlier = (ranks[None, :] < ranks[:, None]).astype(jnp.int32)
    first_live = first * live_col
    second_live = second * live_col
    place_one = jnp.sum(
        jnp.dot(earlier, first_live, preferred_element_type=jnp.int32) * first, axis=1
    )
    ahead = (
        jnp.dot(earlier, second_live, preferred_element_type=jnp.int32)
        + jnp.sum(first_live, axis=0)[None, :]
    )
    place_two = jnp.sum(ahead * second, axis=1)
    keep_one = (live > 0) & (place_one < capacity)
    keep_two = (live > 0) & (place_two < capacity)
    dummy = expert_count * capacity
    slot_one = jnp.where(keep_one, picks[:, 0] * capacity + place_one, dummy)
    slot_two = jnp.where(keep_two, picks[:, 1] * capacity + place_two, dummy)
    pick_one = (first * keep_one[:, None].astype(jnp.int32)).astype(jnp.float32)
    pick_two = (second * keep_two[:, None].astype(jnp.int32)).astype(jnp.float32)
    return (slot_one, slot_two, pick_one, pick_two)


def visible(group, live):
    rows = group.shape[0]
    index = lax.broadcasted_iota(jnp.int32, (rows, rows), 0)
    other = lax.broadcasted_iota(jnp.int32, (rows, rows), 1)
    return (group[:, None] == group[None, :]) & ((live[None, :] > 0) | (index == other))


def attend_forward(query, key, value, allowed, factor):
    scores = jnp.einsum("qhd,khd->hqk", query, key, preferred_element_type=jnp.float32) * factor
    masked = jnp.where(allowed[None], scores, NEGATIVE)
    top = jnp.max(masked, axis=-1, keepdims=True)
    weights = jnp.exp(masked - top)
    total = jnp.sum(weights, axis=-1, keepdims=True)
    probs = (weights / total).astype(jnp.bfloat16)
    mixed = jnp.einsum("hqk,khd->qhd", probs, value, preferred_element_type=jnp.float32)
    return (mixed, top + jnp.log(total))


def attend_backward(query, key, value, allowed, log_total, grad_mixed, factor):
    scores = jnp.einsum("qhd,khd->hqk", query, key, preferred_element_type=jnp.float32) * factor
    masked = jnp.where(allowed[None], scores, NEGATIVE)
    probs = jnp.exp(masked - log_total)
    grad_value = jnp.einsum(
        "hqk,qhd->khd", probs.astype(jnp.bfloat16), grad_mixed, preferred_element_type=jnp.float32
    )
    grad_probs = jnp.einsum("qhd,khd->hqk", grad_mixed, value, preferred_element_type=jnp.float32)
    delta = jnp.sum(probs * grad_probs, axis=-1, keepdims=True)
    grad_scores = (probs * (grad_probs - delta)).astype(jnp.bfloat16)
    grad_query = (
        jnp.einsum("hqk,khd->qhd", grad_scores, key, preferred_element_type=jnp.float32) * factor
    )
    grad_key = (
        jnp.einsum("hqk,qhd->khd", grad_scores, query, preferred_element_type=jnp.float32) * factor
    )
    return jnp.stack([grad_query, grad_key, grad_value], axis=1)


def per_device(
    tokens,
    segments,
    patch_mask,
    choices,
    priority,
    first_gain,
    joint_weight,
    output_weight,
    second_gain,
    router_weight,
    expert_up,
    expert_down,
    out_grad,
):
    row_count, width = tokens.shape
    head_size = width // HEADS
    factor = head_size ** (-0.5)
    expert_count = router_weight.shape[1]
    length = segments.shape[1]
    capacity = (21 * choices.shape[1] * row_count + 20 * expert_count - 1) // (20 * expert_count)
    block_rows = min(row_count, 512)
    gain_one, joint_full, output_full, gain_two, router_full = (
        lax.all_gather(first_gain, ("grp", "ep"), axis=0, tiled=True),
        lax.all_gather(joint_weight, ("grp", "ep"), axis=0, tiled=True),
        lax.all_gather(output_weight, ("grp", "ep"), axis=0, tiled=True),
        lax.all_gather(second_gain, ("grp", "ep"), axis=0, tiled=True),
        lax.all_gather(router_weight, ("grp", "ep"), axis=0, tiled=True),
    )
    inputs = tokens.astype(jnp.float32)
    gain_one = gain_one.astype(jnp.float32)
    gain_two = gain_two.astype(jnp.float32)
    normed_f, unit_one, inverse_one = normalize(inputs, gain_one)
    normed = normed_f.astype(jnp.bfloat16)
    joint = jnp.dot(normed, joint_full, preferred_element_type=jnp.float32).astype(jnp.bfloat16)
    joint = joint.reshape(row_count, 3, HEADS, head_size)
    live = patch_mask.reshape(row_count)
    position = lax.broadcasted_iota(jnp.int32, (row_count,), 0)
    group = position // length * length + segments.reshape(row_count)
    masks = []
    mixed_parts = []
    log_parts = []
    for start in range(0, row_count, block_rows):
        allowed = visible(group[start : start + block_rows], live[start : start + block_rows])
        block = joint[start : start + block_rows]
        mixed_block, log_total = attend_forward(
            block[:, 0], block[:, 1], block[:, 2], allowed, factor
        )
        masks.append(allowed)
        mixed_parts.append(mixed_block)
        log_parts.append(log_total)
    mixed = jnp.concatenate(mixed_parts, axis=0).reshape(row_count, width).astype(jnp.bfloat16)
    state = inputs + jnp.dot(mixed, output_full, preferred_element_type=jnp.float32)
    normed_two_f, unit_two, inverse_two = normalize(state, gain_two)
    normed_two = normed_two_f.astype(jnp.bfloat16)
    logits = jnp.dot(normed_two, router_full, preferred_element_type=jnp.float32)
    gate = jax.nn.softmax(logits, axis=-1)
    slot_one, slot_two, pick_one, pick_two = route(
        choices, live, priority.reshape(row_count), expert_count, capacity
    )
    gate_one = jnp.sum(gate * pick_one, axis=1)
    gate_two = jnp.sum(gate * pick_two, axis=1)
    empty = jnp.zeros((expert_count * capacity + 1, width), jnp.bfloat16)
    outgoing = empty.at[slot_one].add(normed_two).at[slot_two].add(normed_two)
    outgoing = outgoing[: expert_count * capacity].reshape(expert_count, capacity, width)
    arrived = lax.all_to_all(outgoing, "ep", split_axis=0, concat_axis=1, tiled=True)
    pre = jnp.einsum("erd,edf->erf", arrived, expert_up, preferred_element_type=jnp.float32)
    act = jax.nn.gelu(pre, approximate=False).astype(jnp.bfloat16)
    produced = jnp.einsum(
        "erf,efd->erd", act, expert_down, preferred_element_type=jnp.float32
    ).astype(jnp.bfloat16)
    returned = lax.all_to_all(produced, "ep", split_axis=1, concat_axis=0, tiled=True)
    zero_row = jnp.zeros((1, width), jnp.bfloat16)
    flat = jnp.concatenate([returned.reshape(expert_count * capacity, width), zero_row], axis=0)
    got_one = flat[slot_one].astype(jnp.float32)
    got_two = flat[slot_two].astype(jnp.float32)
    output = (state + gate_one[:, None] * got_one + gate_two[:, None] * got_two).astype(
        jnp.bfloat16
    )
    grad = out_grad.astype(jnp.float32)
    grad_gate = (
        pick_one * jnp.sum(grad * got_one, axis=1)[:, None]
        + pick_two * jnp.sum(grad * got_two, axis=1)[:, None]
    )
    grad_logits = (gate * (grad_gate - jnp.sum(gate * grad_gate, axis=1, keepdims=True))).astype(
        jnp.bfloat16
    )
    grad_router = outer(normed_two, grad_logits)
    grad_normed_two = times_t(grad_logits, router_full)
    weighted_one = (gate_one[:, None] * grad).astype(jnp.bfloat16)
    weighted_two = (gate_two[:, None] * grad).astype(jnp.bfloat16)
    grad_out_rows = empty.at[slot_one].add(weighted_one).at[slot_two].add(weighted_two)
    grad_out_rows = grad_out_rows[: expert_count * capacity].reshape(expert_count, capacity, width)
    grad_arrived = lax.all_to_all(grad_out_rows, "ep", split_axis=0, concat_axis=1, tiled=True)
    rows_now = lax.all_to_all(outgoing, "ep", split_axis=0, concat_axis=1, tiled=True)
    pre_now = jnp.einsum("erd,edf->erf", rows_now, expert_up, preferred_element_type=jnp.float32)
    act_now = jax.nn.gelu(pre_now, approximate=False).astype(jnp.bfloat16)
    grad_down = jnp.einsum(
        "erf,erd->efd", act_now, grad_arrived, preferred_element_type=jnp.float32
    )
    grad_act = jnp.einsum(
        "erd,efd->erf", grad_arrived, expert_down, preferred_element_type=jnp.float32
    )
    grad_pre = (grad_act * gelu_slope(pre_now)).astype(jnp.bfloat16)
    grad_up = jnp.einsum("erd,erf->edf", rows_now, grad_pre, preferred_element_type=jnp.float32)
    grad_rows = jnp.einsum(
        "erf,edf->erd", grad_pre, expert_up, preferred_element_type=jnp.float32
    ).astype(jnp.bfloat16)
    grad_back = lax.all_to_all(grad_rows, "ep", split_axis=1, concat_axis=0, tiled=True)
    flat_grad = jnp.concatenate(
        [grad_back.reshape(expert_count * capacity, width), zero_row], axis=0
    )
    grad_normed_two = (
        grad_normed_two
        + flat_grad[slot_one].astype(jnp.float32)
        + flat_grad[slot_two].astype(jnp.float32)
    )
    grad_state_in, grad_gain_two = normalize_back(grad_normed_two, gain_two, unit_two, inverse_two)
    grad_state = grad + grad_state_in
    grad_branch = grad_state.astype(jnp.bfloat16)
    grad_output_w = outer(mixed, grad_branch)
    grad_mixed = (
        times_t(grad_branch, output_full).astype(jnp.bfloat16).reshape(row_count, HEADS, head_size)
    )
    grad_parts = []
    for number, start in enumerate(range(0, row_count, block_rows)):
        block = joint[start : start + block_rows]
        grad_parts.append(
            attend_backward(
                block[:, 0],
                block[:, 1],
                block[:, 2],
                masks[number],
                log_parts[number],
                grad_mixed[start : start + block_rows],
                factor,
            )
        )
    grad_joint = (
        jnp.concatenate(grad_parts, axis=0).reshape(row_count, 3 * width).astype(jnp.bfloat16)
    )
    grad_joint_w = outer(normed, grad_joint)
    grad_normed = times_t(grad_joint, joint_full)
    grad_inputs_in, grad_gain_one = normalize_back(grad_normed, gain_one, unit_one, inverse_one)
    tokens_grad = grad_state + grad_inputs_in
    shares = (
        lax.psum_scatter(grad_gain_one, ("grp", "ep"), scatter_dimension=0, tiled=True),
        lax.psum_scatter(grad_joint_w, ("grp", "ep"), scatter_dimension=0, tiled=True),
        lax.psum_scatter(grad_output_w, ("grp", "ep"), scatter_dimension=0, tiled=True),
        lax.psum_scatter(grad_gain_two, ("grp", "ep"), scatter_dimension=0, tiled=True),
        lax.psum_scatter(grad_router, ("grp", "ep"), scatter_dimension=0, tiled=True),
    )
    grad_up, grad_down = (
        lax.psum(grad_up.astype(jnp.bfloat16), "grp").astype(jnp.float32),
        lax.psum(grad_down.astype(jnp.bfloat16), "grp").astype(jnp.float32),
    )
    return (
        output,
        tokens_grad,
        shares[0],
        shares[1],
        shares[2],
        shares[3],
        shares[4],
        grad_up,
        grad_down,
    )


def solution(mesh):
    in_specs = (
        P(("grp", "ep"), None),
        P(("grp", "ep"), None),
        P(("grp", "ep"), None),
        P(("grp", "ep"), None),
        P(("grp", "ep"), None),
        P(("grp", "ep")),
        P(("grp", "ep"), None),
        P(("grp", "ep"), None),
        P(("grp", "ep")),
        P(("grp", "ep"), None),
        P("ep", None, None),
        P("ep", None, None),
        P(("grp", "ep"), None),
    )
    out_specs = (
        P(("grp", "ep"), None),
        P(("grp", "ep"), None),
        P(("grp", "ep")),
        P(("grp", "ep"), None),
        P(("grp", "ep"), None),
        P(("grp", "ep")),
        P(("grp", "ep"), None),
        P("ep", None, None),
        P("ep", None, None),
    )
    return jax.shard_map(
        per_device, mesh=mesh, in_specs=in_specs, out_specs=out_specs, check_vma=False
    )
```

profile of v0, /device:TPU:0, one launch (start us, length us, event | category | flops | bytes accessed | tf_op | source)
XLA Modules:
  0.0 1114.1 jit_solution(8089762748541029859)
XLA Ops:
  11.2 42.1 %all-reduce.7 = (bf16[512]{0:T(512)(128)(2,1)S(1)}, bf16[512]{0:T(512)(128)(2,1)S(1)}) all-reduce(bf16[512]{0:T(512)(128)(2,1)S(1)} %dynamic-update-slice, bf16[512]{0:T(512)(128)(2,1)S(1)} %dynamic-update-slice.1), channel_id=1, replica_groups=mesh['grp'=4,'ep'=8] {'grp','ep'}, use_global_device_ids=true, to_apply=%add.2 | all-reduce | flops 1024 | bytes 4096
  65.6 74.1 %all_gather.17 = bf16[512,512]{1,0:T(8,128)(2,1)} all-gather(bf16[16,512]{1,0:T(8,128)(2,1)S(1)} %copy-done.51), channel_id=1, replica_groups=mesh['grp'=4,'ep'=8] {'grp','ep'}, dimensions={0}, use_global_device_ids=true | all-gather | bytes 540672 | tf_op jit(solution)/shard_map/all_gather | solution.py:136
  173.4 9.2 scatter_custom_fusion
  182.6 10.6 scatter_fusion
  200.0 53.0 %all_to_all.16 = bf16[8,269,512]{2,1,0:T(8,128)(2,1)} all-to-all(bf16[8,269,512]{2,1,0:T(8,128)(2,1)} %reshape.421), channel_id=1, replica_groups=mesh['grp'=4,'ep'=8] {'ep'}, dimensions={0} | all-to-all | bytes 4407296 | tf_op jit(solution)/shard_map/all_to_all | solution.py:176
  256.7 43.5 %fusion.2 = (bf16[2152,2048]{1,0:T(8,128)(2,1)S(1)}, f32[2152,2048]{1,0:T(8,128)}) fusion(bf16[2152,512]{1,0:T(8,128)(2,1)} %reshape.422, bf16[1,512,2048]{2,1,0:T(8,128)(2,1)S(1)} %copy-done), kind=kOutput, calls=%fused_computation.12 | convolution fusion | flops 4799545344 | bytes 30744576 | tf_op jit(solution)/shard_map/erd,edf->erf/dot_general | solution.py:177
  300.2 5.7 fusion.32
  305.9 16.4 %copy.139 = bf16[1,2152,512]{2,0,1:T(2,128)(2,1)} copy(bf16[1,2152,512]{2,1,0:T(8,128)(2,1)S(1)} %fusion.32) | data formatting | bytes 4407296 | tf_op jit(solution)/shard_map/convert_element_type | solution.py:181
  322.8 16.5 %reduce = bf16[2152,512]{1,0:T(8,128)(2,1)} reduce(bf16[2152,1,512]{2,1,0:T(2,128)(2,1)} %bitcast.160, bf16[]{:T(256)} %broadcast.495), dimensions={1}, to_apply=%bitcast.153.reduce_sub_computation | reduce | bytes 4407298
  349.1 102.5 %all-gather = bf16[32,16,8]{1,2,0:T(8,128)(2,1)S(1)} all-gather(bf16[1,16,8]{1,2,0:T(8,128)(2,1)S(1)} %bitcast.205), channel_id=1, replica_groups=mesh['grp'=4,'ep'=8] {'grp','ep'}, dimensions={0}, use_global_device_ids=true | all-gather | bytes 8448 | tf_op jit(solution)/shard_map/all_gather | solution.py:138
  453.4 7.9 reshape.506
  465.7 7.0 gather_fusion.1
  474.9 7.0 gather_fusion
  492.9 9.0 scatter_custom_fusion.2
  501.9 10.6 scatter_fusion.1
  519.3 52.0 %all_to_all.17 = bf16[8,269,512]{2,1,0:T(8,128)(2,1)} all-to-all(bf16[8,269,512]{2,1,0:T(8,128)(2,1)} %reshape.426), channel_id=1, replica_groups=mesh['grp'=4,'ep'=8] {'ep'}, dimensions={0} | all-to-all | bytes 4407296 | tf_op jit(solution)/shard_map/all_to_all | solution.py:204
  574.9 13.4 %fusion.8 = bf16[2152,2048]{1,0:T(8,128)(2,1)S(1)} fusion(f32[2152,2048]{1,0:T(8,128)} %get-tuple-element.87, bf16[2152,512]{1,0:T(8,128)(2,1)} %reshape.427, bf16[1,2048,512]{2,1,0:T(8,128)(2,1)} %param.24), kind=kOutput, calls=%fused_computation.18 | convolution fusion | flops 4557144064 | bytes 30744576 | tf_op jit(solution)/shard_map/erd,efd->erf/dot_general | solution.py:211
  588.3 5.3 fusion.33
  593.7 16.4 %copy.138 = bf16[1,2152,512]{2,0,1:T(2,128)(2,1)} copy(bf16[1,2152,512]{2,1,0:T(8,128)(2,1)S(1)} %fusion.33) | data formatting | bytes 4407296 | tf_op jit(solution)/shard_map/convert_element_type | solution.py:218
  610.1 16.1 %reduce.1 = bf16[2152,512]{1,0:T(8,128)(2,1)} reduce(bf16[2152,1,512]{2,1,0:T(2,128)(2,1)} %bitcast.161, bf16[]{:T(256)} %broadcast.495), dimensions={1}, to_apply=%bitcast.152.reduce_sub_computation | reduce | bytes 4407298
  637.0 9.8 fusion.35
  646.9 9.9 fusion.34
  656.8 26.4 %all-to-all-done.3 = bf16[8,2,68864]{2,1,0:T(2,128)(2,1)} async-done(((bf16[8,2,68864]{2,1,0:T(2,128)(2,1)}), bf16[8,2,68864]{2,1,0:T(2,128)(2,1)}, u32[]{:S(2)}, u32[]{:S(2)}) %all-to-all-start.3) | async-done | bytes 2203680 | tf_op jit(solution)/shard_map/all_to_all | solution.py:219
  683.2 7.9 reshape.508
  695.5 7.0 gather_fusion.2
  702.6 7.0 gather_fusion.3
  732.9 5.6 multiply_reduce_fusion
  765.7 12.3 %reduce-scatter.10.cloned.1.call-done = f32[16,8]{1,0:T(8,128)} async-done(((f32[512,8]{1,0:T(8,128)}), f32[16,8]{1,0:T(8,128)}) %reduce-scatter.10.cloned.1.call-update) | async-done | bytes 528
  779.4 85.5 %all-reduce.11.cloned.1.call-done = (bf16[1,512,2048]{2,1,0:T(8,128)(2,1)}, bf16[1,2048,512]{2,1,0:T(8,128)(2,1)}) async-done(((bf16[1,512,2048]{2,1,0:T(8,128)(2,1)}, bf16[1,2048,512]{2,1,0:T(8,128)(2,1)}), (bf16[1,512,2048]{2,1,0:T(8,128)(2,1)}, bf16[1,2048,512]{2,1,0:T(8,128)(2,1)})) %all-reduce.11.cloned.1.call-update) | async-done | bytes 4194320 | tf_op jit(solution)/shard_map/psum | solution.py:264
  876.5 39.7 %all-reduce.6 = (f32[512]{0:T(512)S(1)}, f32[512]{0:T(512)S(1)}) all-reduce(f32[512]{0:T(512)S(1)} %get-tuple-element.47, f32[512]{0:T(512)S(1)} %get-tuple-element.45), channel_id=2, replica_groups=mesh['grp'=4,'ep'=8] {'grp','ep'}, use_global_device_ids=true, to_apply=%region_29.30.clone | all-reduce | flops 1024 | bytes 8192
  925.9 77.0 %reduce-scatter.8.cloned.1.call-done = f32[16,512]{1,0:T(8,128)} async-done(((f32[512,512]{1,0:T(8,128)}), f32[16,512]{1,0:T(8,128)}) %reduce-scatter.8.cloned.1.call-update) | async-done | bytes 32784 | tf_op jit(solution)/shard_map/reduce_scatter | solution.py:259
  1002.9 104.5 %reduce-scatter.6.cloned.1.call-done = f32[16,1536]{1,0:T(8,128)} async-done(((f32[512,1536]{1,0:T(8,128)}), f32[16,1536]{1,0:T(8,128)}) %reduce-scatter.6.cloned.1.call-update) | async-done | bytes 98320 | tf_op jit(solution)/shard_map/reduce_scatter | solution.py:258
  (261 shorter events, 187.9 us)
Async XLA Ops:
  7.2 249.5 %copy-start = (bf16[1,512,2048]{2,1,0:T(8,128)(2,1)S(1)}, bf16[1,512,2048]{2,1,0:T(8,128)(2,1)}, u32[]{:S(2)}) copy-start(bf16[1,512,2048]{2,1,0:T(8,128)(2,1)} %param.23) | copy-start | bytes 6291460
  7.2 57.0 %copy-start.46 = (s32[1024,2]{0,1:T(2,128)S(1)}, s32[1024,2]{0,1:T(2,128)}, u32[]{:S(2)}) copy-start(s32[1024,2]{0,1:T(2,128)} %param.16) | copy-start | bytes 24580
  7.2 58.4 %copy-start.51 = (bf16[16,512]{1,0:T(8,128)(2,1)S(1)}, bf16[16,512]{1,0:T(8,128)(2,1)}, u32[]{:S(2)}) copy-start(bf16[16,512]{1,0:T(8,128)(2,1)} %param.20) | copy-start | bytes 49156
  7.2 132.5 %all-gather.3.cloned.1.call-start = ((), (), s32[]{:S(2)}) async-start(), calls=%async_computation.7 | async-start | bytes 1622016 | tf_op jit(solution)/shard_map/all_gather | solution.py:135
  9.5 159.7 %copy-start.7 = (bf16[1024,512]{0,1:T(8,128)(2,1)}, bf16[1024,512]{0,1:T(8,128)(2,1)S(1)}, u32[]{:S(2)}) copy-start(bf16[1024,512]{0,1:T(8,128)(2,1)S(1)} %copy.92) | copy-start | bytes 3145732
  53.3 89.8 %copy-start.58 = (f32[512]{0:T(512)}, f32[512]{0:T(512)S(1)}, u32[]{:S(2)}) copy-start(f32[512]{0:T(512)S(1)} %convert_element_type.142) | copy-start | bytes 6148
  54.8 115.5 %copy-start.47 = (f32[512]{0:T(512)}, f32[512]{0:T(512)S(1)}, u32[]{:S(2)}) copy-start(f32[512]{0:T(512)S(1)} %convert_element_type.148) | copy-start | bytes 6148
  55.5 8.7 copy-start.42
  57.0 7.2 copy-start.38
  57.0 8.6 copy-start.44
  63.8 79.3 %copy-start.40 = (f32[1024]{0:T(1024)}, f32[1024]{0:T(1024)S(1)}, u32[]{:S(2)}) copy-start(f32[1024]{0:T(1024)S(1)} %broadcast_multiply_fusion.5) | copy-start | bytes 12292
  64.1 79.0 %copy-start.49 = (f32[1024]{0:T(1024)}, f32[1024]{0:T(1024)S(1)}, u32[]{:S(2)}) copy-start(f32[1024]{0:T(1024)S(1)} %add_rsqrt_fusion.1) | copy-start | bytes 12292
  64.2 109.2 %copy-start.52 = (s32[1024,1]{0,1:T(1,128)}, s32[1024,1]{0,1:T(1,128)S(1)}, u32[]{:S(2)}) copy-start(s32[1024,1]{0,1:T(1,128)S(1)} %get-tuple-element.73) | copy-start | bytes 12292
  172.1 21.1 %copy-start.9 = (bf16[1024,512]{0,1:T(8,128)(2,1)}, bf16[1024,512]{0,1:T(8,128)(2,1)S(1)}, u32[]{:S(2)}) copy-start(bf16[1024,512]{0,1:T(8,128)(2,1)S(1)} %multiply_convert_fusion.2) | copy-start | bytes 3145732
  256.7 43.5 %copy-start.61 = (bf16[1,2048,512]{2,1,0:T(8,128)(2,1)S(1)}, bf16[1,2048,512]{2,1,0:T(8,128)(2,1)}, u32[]{:S(2)}) copy-start(bf16[1,2048,512]{2,1,0:T(8,128)(2,1)} %param.24) | copy-start | bytes 6291460
  343.2 108.5 %copy-start.53 = (s32[1024,1]{0,1:T(1,128)S(1)}, s32[1024,1]{0,1:T(1,128)}, u32[]{:S(2)}) copy-start(s32[1024,1]{0,1:T(1,128)} %copy-done.52) | copy-start | bytes 12292
  343.2 108.6 %copy-start.43 = (s32[1,2,4,128]{3,1,2,0:T(2,128)S(1)}, s32[1,2,4,128]{3,1,2,0:T(2,128)}, u32[]{:S(2)}) copy-start(s32[1,2,4,128]{3,1,2,0:T(2,128)} %copy-done.42) | copy-start | bytes 12292
  343.2 108.6 %copy-start.55 = (s32[1024]{0:T(1024)S(1)}, s32[1024]{0:T(1024)}, u32[]{:S(2)}) copy-start(s32[1024]{0:T(1024)} %copy-done.54) | copy-start | bytes 12292
  343.2 108.6 %copy-start.57 = (s32[1024]{0:T(1024)S(1)}, s32[1024]{0:T(1024)}, u32[]{:S(2)}) copy-start(s32[1024]{0:T(1024)} %copy-done.56) | copy-start | bytes 12292
  343.2 110.1 %all-to-all-start.1 = ((bf16[8,2,68864]{2,1,0:T(2,128)(2,1)}), bf16[8,2,68864]{2,1,0:T(2,128)(2,1)}, u32[]{:S(2)}, u32[]{:S(2)}) async-start(bf16[8,2,68864]{2,1,0:T(2,128)(2,1)} %reshape.505), calls=%async_computation.1 | async-start | bytes 4407296 | tf_op jit(solution)/shard_map/all_to_all | solution.py:182
  626.2 8.4 copy-start.27
  626.2 8.4 copy-start.35
  626.2 8.4 copy-start.29
  626.2 8.4 copy-start.37
  630.1 53.2 %all-to-all-start.3 = ((bf16[8,2,68864]{2,1,0:T(2,128)(2,1)}), bf16[8,2,68864]{2,1,0:T(2,128)(2,1)}, u32[]{:S(2)}, u32[]{:S(2)}) async-start(bf16[8,2,68864]{2,1,0:T(2,128)(2,1)} %reshape.507), calls=%async_computation.3 | async-start | bytes 4407296 | tf_op jit(solution)/shard_map/all_to_all | solution.py:219
  634.5 143.6 %reduce-scatter.10.cloned.1.call-start = ((), (), s32[]{:S(2)}) async-start(), calls=%async_computation.10 | async-start | bytes 270336
  637.0 227.9 %all-reduce.11.cloned.1.call-start = ((), (), s32[]{:S(2)}) async-start(), calls=%async_computation.11 | async-start | bytes 8388608 | tf_op jit(solution)/shard_map/psum | solution.py:264
  637.0 9.8 copy-start.20
  656.8 346.1 %reduce-scatter.8.cloned.1.call-start = ((), (), s32[]{:S(2)}) async-start(), calls=%async_computation.9 | async-start | bytes 1081344 | tf_op jit(solution)/shard_map/reduce_scatter | solution.py:259
  720.0 11.2 %copy-start.6 = (f32[1024,512]{0,1:T(8,128)}, f32[1024,512]{0,1:T(8,128)S(1)}, u32[]{:S(2)}) copy-start(f32[1024,512]{0,1:T(8,128)S(1)} %get-tuple-element.66) | copy-start | bytes 6291460
  732.9 6.0 slice-start.3
  746.4 361.0 %reduce-scatter.6.cloned.1.call-start = ((), (), s32[]{:S(2)}) async-start(), calls=%async_computation.8 | async-start | bytes 3244032 | tf_op jit(solution)/shard_map/reduce_scatter | solution.py:258
  (44 other events, 147.3 us)
Sparse Core Ops, SparseCore 0:
  10.9 57.7 all-gather.2
  637.5 140.4 reduce-scatter.9
  781.2 83.6 all-reduce.10
  867.6 135.2 reduce-scatter.7
  1009.6 97.7 reduce-scatter.5
where the time goes:
time: 1120 us; the launch traced here: 1110 us
  blocking collectives  363 us (32%)
  waiting for transfers between devices  307 us (27%)
  local copies, waits for them, and re-layouts  164 us (15%)
  matrix products  154 us (14%)
  other arithmetic  102 us (9%)
  between operations  15 us (1%)
    reduce_scatter x1, waiting for transfers between devices, per_device(): lax.psum_scatter(grad_joint_w, ('grp', 'ep'), scatter_dimension=0, tiled=...  105 us
    all_gather x1, blocking collectives, per_device(): lax.all_gather(router_weight, ('grp', 'ep'), axis=0, tiled=True)  102 us
    psum x1, waiting for transfers between devices, per_device(): lax.psum(grad_up.astype(jnp.bfloat16), 'grp').astype(jnp.float32)  85.5 us
    unnamed x2, blocking collectives  81.8 us
    reduce_scatter x1, waiting for transfers between devices, per_device(): lax.psum_scatter(grad_output_w, ('grp', 'ep'), scatter_dimension=0, tiled...  77 us
    all_gather x1, blocking collectives, per_device(): lax.all_gather(output_weight, ('grp', 'ep'), axis=0, tiled=True)  74.1 us
    unnamed x160, local copies, waits for them, and re-layouts  56.1 us
    all_to_all x1, blocking collectives, per_device(): lax.all_to_all(outgoing, 'ep', split_axis=0, concat_axis=1, tiled=True)  53 us
  transfers between devices with their start and end apart: 7, of which 5 were waited for; matrix products, arithmetic and copies ran while one was open for 12% of the time, Pallas kernels for 0%

commit v1 on v0

--- a/solution.py
+++ b/solution.py
@@ -6,6 +6,22 @@
 HEADS = 8
 EPSILON = 1e-06
 NEGATIVE = -1e30
+
+
+def exchange_in_pairs(value, axis, split, join):
+    ways, here = (lax.axis_size(axis), lax.axis_index(axis))
+    width = value.shape[split] // ways
+    shape = list(value.shape)
+    shape[split] = width
+    height = shape[join]
+    shape[join] = height * ways
+    full = jnp.zeros(shape, value.dtype)
+    for mask in range(ways):
+        part = lax.dynamic_slice_in_dim(value, (here ^ mask) * width, width, axis=split)
+        if mask:
+            part = lax.ppermute(part, axis, [(d, d ^ mask) for d in range(ways)])
+        full = lax.dynamic_update_slice_in_dim(full, part, (here ^ mask) * height, axis=join)
+    return full
 
 
 def normalize(values, gain):
@@ -216,7 +232,7 @@
     grad_rows = jnp.einsum(
         "erf,edf->erd", grad_pre, expert_up, preferred_element_type=jnp.float32
     ).astype(jnp.bfloat16)
-    grad_back = lax.all_to_all(grad_rows, "ep", split_axis=1, concat_axis=0, tiled=True)
+    grad_back = exchange_in_pairs(grad_rows, "ep", 1, 0)
     flat_grad = jnp.concatenate(
         [grad_back.reshape(expert_count * capacity, width), zero_row], axis=0
     )

time: 1120 us -> 1020 us (0.911)
  blocking collectives: 363 us -> 317 us
  waiting for transfers between devices: 307 us -> 267 us
  other arithmetic: 102 us -> 90.1 us
  starting transfers between devices: 8.95 us -> 20.4 us
    psum x1, waiting for transfers between devices: 85.5 us -> 0.01 us  [per_device(): lax.psum(grad_up.astype(jnp.bfloat16), 'grp').astype(jnp.float32)]
    all_to_all x1 -> x0, blocking collectives: 52 us -> none  [per_device(): lax.all_to_all(grad_out_rows, 'ep', split_axis=0, concat_axis=1, tiled=True)]
    ppermute x0 -> x7, waiting for transfers between devices: none -> 24.2 us  [exchange_in_pairs(): part = lax.ppermute(part, axis, [(d, d ^ mask) for d in range(ways)])]
    all_to_all x1, waiting for transfers between devices: 26.4 us -> 43.5 us  [per_device(): lax.all_to_all(grad_out_rows, 'ep', split_axis=0, concat_axis=1, tiled=True)]
    reduce_scatter x1, waiting for transfers between devices: 77 us -> 93.8 us  [per_device(): lax.psum_scatter(grad_output_w, ('grp', 'ep'), scatter_dimension=0, tiled...]
    convert_element_type x1 -> x0, local copies, waits for them, and re-layouts: 16.4 us -> none  [per_device(): grad_rows = jnp.einsum('erf,edf->erd', grad_pre, expert_up, preferred_ele...]
    unnamed x5 -> x4, other arithmetic: 33.3 us -> 17.2 us
    unnamed x160 -> x159, local copies, waits for them, and re-layouts: 56.1 us -> 41.6 us
  transfers between devices with their start and end apart: 7 -> 14, of which waited for: 5 -> 5; matrix products, arithmetic and copies ran while one was open for 12% -> 17% of each run, Pallas kernels for 0% -> 0%
where the time goes in v1:
time: 1020 us; the launch traced here: 1010 us
  blocking collectives  317 us (31%)
  waiting for transfers between devices  267 us (26%)
  local copies, waits for them, and re-layouts  153 us (15%)
  matrix products  149 us (15%)
  other arithmetic  90.1 us (9%)
  starting transfers between devices  20.4 us (2%)
  between operations  15 us (1%)
    reduce_scatter x1, waiting for transfers between devices, per_device(): lax.psum_scatter(grad_joint_w, ('grp', 'ep'), scatter_dimension=0, tiled=...  105 us
    all_gather x1, blocking collectives, per_device(): lax.all_gather(router_weight, ('grp', 'ep'), axis=0, tiled=True)  102 us
    reduce_scatter x1, waiting for transfers between devices, per_device(): lax.psum_scatter(grad_output_w, ('grp', 'ep'), scatter_dimension=0, tiled...  93.8 us
    unnamed x2, blocking collectives  87.6 us
    all_gather x1, blocking collectives, per_device(): lax.all_gather(output_weight, ('grp', 'ep'), axis=0, tiled=True)  74 us
    all_to_all x1, blocking collectives, per_device(): lax.all_to_all(outgoing, 'ep', split_axis=0, concat_axis=1, tiled=True)  53 us
    dot_general x1, matrix products, per_device(): jnp.einsum('erd,edf->erf', arrived, expert_up, preferred_element_type=jnp...  43.5 us
    all_to_all x1, waiting for transfers between devices, per_device(): lax.all_to_all(grad_out_rows, 'ep', split_axis=0, concat_axis=1, tiled=True)  43.5 us
  transfers between devices with their start and end apart: 14, of which 5 were waited for; matrix products, arithmetic and copies ran while one was open for 17% of the time, Pallas kernels for 0%

profile of v1, /device:TPU:0, one launch (start us, length us, event | category | flops | bytes accessed | tf_op | source)
XLA Modules:
  0.0 1012.3 jit_solution(11128390026188751053)
XLA Ops:
  11.2 42.1 %all-reduce.7 = (bf16[512]{0:T(512)(128)(2,1)S(1)}, bf16[512]{0:T(512)(128)(2,1)S(1)}) all-reduce(bf16[512]{0:T(512)(128)(2,1)S(1)} %dynamic-update-slice, bf16[512]{0:T(512)(128)(2,1)S(1)} %dynamic-update-slice.1), channel_id=1, replica_groups=mesh['grp'=4,'ep'=8] {'grp','ep'}, use_global_device_ids=true, to_apply=%add.2 | all-reduce | flops 1024 | bytes 4096
  64.9 74.0 %all_gather.17 = bf16[512,512]{1,0:T(8,128)(2,1)} all-gather(bf16[16,512]{1,0:T(8,128)(2,1)S(1)} %copy-done.52), channel_id=1, replica_groups=mesh['grp'=4,'ep'=8] {'grp','ep'}, dimensions={0}, use_global_device_ids=true | all-gather | bytes 540672 | tf_op jit(solution)/shard_map/all_gather | solution.py:152
  172.4 9.5 scatter_custom_fusion
  181.9 10.6 %scatter_fusion = bf16[2153,512]{1,0:T(8,128)(2,1)} fusion(bf16[2153,512]{1,0:T(8,128)(2,1)} %scatter_custom_fusion, s32[1024]{0:T(1024)S(1)} %bitcast.186, bf16[1024,512]{1,0:T(8,128)(2,1)} %copy.97), kind=kCustom, calls=%fused_computation.5 | custom fusion | flops 524288 | bytes 3149824 | tf_op jit(solution)/shard_map/scatter-add | solution.py:190
  199.3 53.0 %all_to_all.12 = bf16[8,269,512]{2,1,0:T(8,128)(2,1)} all-to-all(bf16[8,269,512]{2,1,0:T(8,128)(2,1)} %reshape.425), channel_id=1, replica_groups=mesh['grp'=4,'ep'=8] {'ep'}, dimensions={0} | all-to-all | bytes 4407296 | tf_op jit(solution)/shard_map/all_to_all | solution.py:192
  256.0 43.5 %fusion.2 = (bf16[2152,2048]{1,0:T(8,128)(2,1)S(1)}, f32[2152,2048]{1,0:T(8,128)}) fusion(bf16[2152,512]{1,0:T(8,128)(2,1)} %reshape.426, bf16[1,512,2048]{2,1,0:T(8,128)(2,1)S(1)} %copy-done), kind=kOutput, calls=%fused_computation.12 | convolution fusion | flops 4799545344 | bytes 30744576 | tf_op jit(solution)/shard_map/erd,edf->erf/dot_general | solution.py:193
  299.5 5.7 fusion.32
  305.2 16.4 %copy.132 = bf16[1,2152,512]{2,0,1:T(2,128)(2,1)} copy(bf16[1,2152,512]{2,1,0:T(8,128)(2,1)S(1)} %fusion.32) | data formatting | bytes 4407296 | tf_op jit(solution)/shard_map/convert_element_type | solution.py:197
  322.2 16.5 %reduce = bf16[2152,512]{1,0:T(8,128)(2,1)} reduce(bf16[2152,1,512]{2,1,0:T(2,128)(2,1)} %bitcast.166, bf16[]{:T(256)} %broadcast.499), dimensions={1}, to_apply=%bitcast.160.reduce_sub_computation | reduce | bytes 4407298
  348.3 102.5 %all-gather = bf16[32,16,8]{1,2,0:T(8,128)(2,1)S(1)} all-gather(bf16[1,16,8]{1,2,0:T(8,128)(2,1)S(1)} %bitcast.209), channel_id=1, replica_groups=mesh['grp'=4,'ep'=8] {'grp','ep'}, dimensions={0}, use_global_device_ids=true | all-gather | bytes 8448 | tf_op jit(solution)/shard_map/all_gather | solution.py:154
  452.6 7.9 reshape.510
  464.9 7.0 gather_fusion.1
  474.2 7.0 gather_fusion
  492.1 9.0 scatter_custom_fusion.2
  501.1 10.8 %scatter_fusion.1 = bf16[2153,512]{1,0:T(8,128)(2,1)} fusion(bf16[2153,512]{1,0:T(8,128)(2,1)} %scatter_custom_fusion.2, s32[1024]{0:T(1024)S(1)} %bitcast.188, bf16[1024,512]{1,0:T(8,128)(2,1)} %copy.104), kind=kCustom, calls=%fused_computation.7 | custom fusion | flops 524288 | bytes 3149824 | tf_op jit(solution)/shard_map/scatter-add | solution.py:218
  518.6 4.5 all-to-all-start.2
  527.6 43.5 %all-to-all-done.2 = bf16[8,269,512]{2,1,0:T(8,128)(2,1)} async-done(((bf16[8,269,512]{2,1,0:T(8,128)(2,1)}), bf16[8,269,512]{2,1,0:T(8,128)(2,1)}, u32[]{:S(2)}, u32[]{:S(2)}) %all-to-all-start.2) | async-done | bytes 2203680 | tf_op jit(solution)/shard_map/all_to_all | solution.py:220
  574.8 9.3 fusion.34
  584.1 12.4 %fusion.8 = bf16[2152,2048]{1,0:T(8,128)(2,1)S(1)} fusion(f32[2152,2048]{1,0:T(8,128)} %get-tuple-element.95, bf16[2152,512]{1,0:T(8,128)(2,1)S(1)} %copy-done.21, bf16[1,2048,512]{2,1,0:T(8,128)(2,1)S(1)} %copy-done.63), kind=kOutput, calls=%fused_computation.18 | convolution fusion | flops 4557144064 | bytes 30744576 | tf_op jit(solution)/shard_map/erd,efd->erf/dot_general | solution.py:227
  596.6 5.3 convolution_convert_fusion
  605.9 6.3 fusion.33
  630.5 18.9 %collective-permute-done.3 = bf16[1,269,512]{2,1,0:T(8,128)(2,1)} collective-permute-done((bf16[1,269,512]{2,1,0:T(8,128)(2,1)}, bf16[1,269,512]{2,1,0:T(8,128)(2,1)}, u32[]{:S(2)}, u32[]{:S(2)}) %collective-permute-start.3) | collective-permute-done | bytes 275488 | tf_op jit(solution)/shard_map/ppermute | solution.py:22
  651.1 5.2 collective-permute-done.4
  666.3 7.4 gather_fusion.2
  673.7 7.0 gather_fusion.3
  704.5 5.7 multiply_reduce_fusion
  721.9 4.9 fusion.83
  726.8 5.3 fusion.80
  739.2 5.8 fusion.46
  745.1 45.6 %all-reduce.6 = (f32[512]{0:T(512)S(1)}, f32[512]{0:T(512)S(1)}) all-reduce(f32[512]{0:T(512)S(1)} %get-tuple-element.47, f32[512]{0:T(512)S(1)} %get-tuple-element.45), channel_id=2, replica_groups=mesh['grp'=4,'ep'=8] {'grp','ep'}, use_global_device_ids=true, to_apply=%region_29.30.clone | all-reduce | flops 1024 | bytes 8192
  807.2 93.8 %reduce-scatter.8.cloned.1.call-done = f32[16,512]{1,0:T(8,128)} async-done(((f32[512,512]{1,0:T(8,128)}), f32[16,512]{1,0:T(8,128)}) %reduce-scatter.8.cloned.1.call-update) | async-done | bytes 32784 | tf_op jit(solution)/shard_map/reduce_scatter | solution.py:275
  900.9 104.7 %reduce-scatter.6.cloned.1.call-done = f32[16,1536]{1,0:T(8,128)} async-done(((f32[512,1536]{1,0:T(8,128)}), f32[16,1536]{1,0:T(8,128)}) %reduce-scatter.6.cloned.1.call-update) | async-done | bytes 98320 | tf_op jit(solution)/shard_map/reduce_scatter | solution.py:274
  (283 shorter events, 195.9 us)
Async XLA Ops:
  7.2 248.8 %copy-start = (bf16[1,512,2048]{2,1,0:T(8,128)(2,1)S(1)}, bf16[1,512,2048]{2,1,0:T(8,128)(2,1)}, u32[]{:S(2)}) copy-start(bf16[1,512,2048]{2,1,0:T(8,128)(2,1)} %param.23) | copy-start | bytes 6291460
  7.2 53.2 %copy-start.64 = (s32[1,1024]{1,0:T(1,128)S(1)}, s32[1,1024]{1,0:T(1,128)}, u32[]{:S(2)}) copy-start(s32[1,1024]{1,0:T(1,128)} %param.17) | copy-start | bytes 12292
  7.2 131.7 %all-gather.3.cloned.1.call-start = ((), (), s32[]{:S(2)}) async-start(), calls=%async_computation.6 | async-start | bytes 1622016 | tf_op jit(solution)/shard_map/all_gather | solution.py:151
  7.9 55.5 %copy-start.47 = (s32[1024,2]{0,1:T(2,128)S(1)}, s32[1024,2]{0,1:T(2,128)}, u32[]{:S(2)}) copy-start(s32[1024,2]{0,1:T(2,128)} %param.16) | copy-start | bytes 24580
  8.0 56.9 %copy-start.52 = (bf16[16,512]{1,0:T(8,128)(2,1)S(1)}, bf16[16,512]{1,0:T(8,128)(2,1)}, u32[]{:S(2)}) copy-start(bf16[16,512]{1,0:T(8,128)(2,1)} %param.20) | copy-start | bytes 49156
  9.5 158.6 %copy-start.7 = (bf16[1024,512]{0,1:T(8,128)(2,1)}, bf16[1024,512]{0,1:T(8,128)(2,1)S(1)}, u32[]{:S(2)}) copy-start(bf16[1024,512]{0,1:T(8,128)(2,1)S(1)} %copy.91) | copy-start | bytes 3145732
  53.3 89.0 %copy-start.59 = (f32[512]{0:T(512)}, f32[512]{0:T(512)S(1)}, u32[]{:S(2)}) copy-start(f32[512]{0:T(512)S(1)} %convert_element_type.140) | copy-start | bytes 6148
  54.8 114.4 %copy-start.48 = (f32[512]{0:T(512)}, f32[512]{0:T(512)S(1)}, u32[]{:S(2)}) copy-start(f32[512]{0:T(512)S(1)} %convert_element_type.146) | copy-start | bytes 6148
  63.1 79.2 %copy-start.41 = (f32[1024]{0:T(1024)}, f32[1024]{0:T(1024)S(1)}, u32[]{:S(2)}) copy-start(f32[1024]{0:T(1024)S(1)} %broadcast_multiply_fusion.5) | copy-start | bytes 12292
  63.4 78.9 %copy-start.50 = (f32[1024]{0:T(1024)}, f32[1024]{0:T(1024)S(1)}, u32[]{:S(2)}) copy-start(f32[1024]{0:T(1024)S(1)} %add_rsqrt_fusion.1) | copy-start | bytes 12292
  63.5 108.9 %copy-start.53 = (s32[1024,1]{0,1:T(1,128)}, s32[1024,1]{0,1:T(1,128)S(1)}, u32[]{:S(2)}) copy-start(s32[1024,1]{0,1:T(1,128)S(1)} %get-tuple-element.81) | copy-start | bytes 12292
  171.1 21.5 %copy-start.9 = (bf16[1024,512]{0,1:T(8,128)(2,1)}, bf16[1024,512]{0,1:T(8,128)(2,1)S(1)}, u32[]{:S(2)}) copy-start(bf16[1024,512]{0,1:T(8,128)(2,1)S(1)} %multiply_convert_fusion.2) | copy-start | bytes 3145732
  256.0 43.5 %copy-start.62 = (bf16[1,2048,512]{2,1,0:T(8,128)(2,1)S(1)}, bf16[1,2048,512]{2,1,0:T(8,128)(2,1)}, u32[]{:S(2)}) copy-start(bf16[1,2048,512]{2,1,0:T(8,128)(2,1)} %param.24) | copy-start | bytes 6291460
  342.4 108.5 %copy-start.54 = (s32[1024,1]{0,1:T(1,128)S(1)}, s32[1024,1]{0,1:T(1,128)}, u32[]{:S(2)}) copy-start(s32[1024,1]{0,1:T(1,128)} %copy-done.53) | copy-start | bytes 12292
  342.4 108.6 %copy-start.44 = (s32[1,2,4,128]{3,1,2,0:T(2,128)S(1)}, s32[1,2,4,128]{3,1,2,0:T(2,128)}, u32[]{:S(2)}) copy-start(s32[1,2,4,128]{3,1,2,0:T(2,128)} %copy-done.43) | copy-start | bytes 12292
  342.4 108.6 %copy-start.56 = (s32[1024]{0:T(1024)S(1)}, s32[1024]{0:T(1024)}, u32[]{:S(2)}) copy-start(s32[1024]{0:T(1024)} %copy-done.55) | copy-start | bytes 12292
  342.4 108.6 %copy-start.58 = (s32[1024]{0:T(1024)S(1)}, s32[1024]{0:T(1024)}, u32[]{:S(2)}) copy-start(s32[1024]{0:T(1024)} %copy-done.57) | copy-start | bytes 12292
  342.4 110.1 %all-to-all-start.1 = ((bf16[8,2,68864]{2,1,0:T(2,128)(2,1)}), bf16[8,2,68864]{2,1,0:T(2,128)(2,1)}, u32[]{:S(2)}, u32[]{:S(2)}) async-start(bf16[8,2,68864]{2,1,0:T(2,128)(2,1)} %reshape.509), calls=%async_computation.1 | async-start | bytes 4407296 | tf_op jit(solution)/shard_map/all_to_all | solution.py:198
  518.6 52.5 %all-to-all-start.2 = ((bf16[8,269,512]{2,1,0:T(8,128)(2,1)}), bf16[8,269,512]{2,1,0:T(8,128)(2,1)}, u32[]{:S(2)}, u32[]{:S(2)}) async-start(bf16[8,269,512]{2,1,0:T(8,128)(2,1)} %reshape.430), calls=%async_computation.2 | async-start | bytes 4456448 | tf_op jit(solution)/shard_map/all_to_all | solution.py:220
  523.1 214.7 %reduce-scatter.10.cloned.1.call-start = ((), (), s32[]{:S(2)}) async-start(), calls=%async_computation.9 | async-start | bytes 270336
  525.7 274.5 %all-reduce.11.cloned.1.call-start = ((), (), s32[]{:S(2)}) async-start(), calls=%async_computation.10 | async-start | bytes 8388608 | tf_op jit(solution)/shard_map/psum | solution.py:280
  574.8 9.3 copy-start.63
  604.7 16.8 %collective-permute-start = (bf16[1,269,512]{2,1,0:T(8,128)(2,1)}, bf16[1,269,512]{2,1,0:T(8,128)(2,1)}, u32[]{:S(2)}, u32[]{:S(2)}) collective-permute-start(bf16[1,269,512]{2,1,0:T(8,128)(2,1)} %get-tuple-element.73), channel_id=1, source_target_pairs={{0,1},{1,0},{2,3},{3,2},{4,5},{5,4},{6,7},{7,6},{8,9},{9,8},{10,11... | collective-permute-start | bytes 826376 | tf_op jit(solution)/shard_map/ppermute | solution.py:22
  605.9 18.7 %collective-permute-start.1 = (bf16[1,269,512]{2,1,0:T(8,128)(2,1)}, bf16[1,269,512]{2,1,0:T(8,128)(2,1)}, u32[]{:S(2)}, u32[]{:S(2)}) collective-permute-start(bf16[1,269,512]{2,1,0:T(8,128)(2,1)} %get-tuple-element.72), channel_id=1, source_target_pairs={{0,2},{1,3},{2,0},{3,1},{4,6},{5,7},{6,4},{7,5},{8,10},{9,11},{10,... | collective-permute-start | bytes 826376 | tf_op jit(solution)/shard_map/ppermute | solution.py:22
  612.2 16.6 %collective-permute-start.2 = (bf16[1,269,512]{2,1,0:T(8,128)(2,1)}, bf16[1,269,512]{2,1,0:T(8,128)(2,1)}, u32[]{:S(2)}, u32[]{:S(2)}) collective-permute-start(bf16[1,269,512]{2,1,0:T(8,128)(2,1)} %get-tuple-element.71), channel_id=1, source_target_pairs={{0,3},{1,2},{2,1},{3,0},{4,7},{5,6},{6,5},{7,4},{8,11},{9,10},{10,... | collective-permute-start | bytes 826376 | tf_op jit(solution)/shard_map/ppermute | solution.py:22
  614.5 35.0 %collective-permute-start.3 = (bf16[1,269,512]{2,1,0:T(8,128)(2,1)}, bf16[1,269,512]{2,1,0:T(8,128)(2,1)}, u32[]{:S(2)}, u32[]{:S(2)}) collective-permute-start(bf16[1,269,512]{2,1,0:T(8,128)(2,1)} %get-tuple-element.70), channel_id=1, source_target_pairs={{0,4},{1,5},{2,6},{3,7},{4,0},{5,1},{6,2},{7,3},{8,12},{9,13},{10,... | collective-permute-start | bytes 826376 | tf_op jit(solution)/shard_map/ppermute | solution.py:22
  614.5 41.9 %collective-permute-start.4 = (bf16[1,269,512]{2,1,0:T(8,128)(2,1)}, bf16[1,269,512]{2,1,0:T(8,128)(2,1)}, u32[]{:S(2)}, u32[]{:S(2)}) collective-permute-start(bf16[1,269,512]{2,1,0:T(8,128)(2,1)} %get-tuple-element.69), channel_id=1, source_target_pairs={{0,5},{1,4},{2,7},{3,6},{4,1},{5,0},{6,3},{7,2},{8,13},{9,12},{10,... | collective-permute-start | bytes 826376 | tf_op jit(solution)/shard_map/ppermute | solution.py:22
  618.1 282.9 %reduce-scatter.8.cloned.1.call-start = ((), (), s32[]{:S(2)}) async-start(), calls=%async_computation.8 | async-start | bytes 1081344 | tf_op jit(solution)/shard_map/reduce_scatter | solution.py:275
  621.4 36.6 %collective-permute-start.5 = (bf16[1,269,512]{2,1,0:T(8,128)(2,1)}, bf16[1,269,512]{2,1,0:T(8,128)(2,1)S(1)}, u32[]{:S(2)}, u32[]{:S(2)}) collective-permute-start(bf16[1,269,512]{2,1,0:T(8,128)(2,1)} %get-tuple-element.68), channel_id=1, source_target_pairs={{0,6},{1,7},{2,4},{3,5},{4,2},{5,3},{6,0},{7,1},{8,14},{9,15},{10,... | collective-permute-start | bytes 826376 | tf_op jit(solution)/shard_map/ppermute | solution.py:22
  624.6 34.2 %collective-permute-start.6 = (bf16[1,269,512]{2,1,0:T(8,128)(2,1)S(1)}, bf16[1,269,512]{2,1,0:T(8,128)(2,1)S(1)}, u32[]{:S(2)}, u32[]{:S(2)}) collective-permute-start(bf16[1,269,512]{2,1,0:T(8,128)(2,1)S(1)} %get-tuple-element.67), channel_id=1, source_target_pairs={{0,7},{1,6},{2,5},{3,4},{4,3},{5,2},{6,1},{7,0},{8,15},{9,14},{10,... | collective-permute-start | bytes 826376 | tf_op jit(solution)/shard_map/ppermute | solution.py:22
  691.7 11.1 %copy-start.6 = (f32[1024,512]{0,1:T(8,128)}, f32[1024,512]{0,1:T(8,128)S(1)}, u32[]{:S(2)}) copy-start(f32[1024,512]{0,1:T(8,128)S(1)} %get-tuple-element.74) | copy-start | bytes 6291460
  717.9 287.7 %reduce-scatter.6.cloned.1.call-start = ((), (), s32[]{:S(2)}) async-start(), calls=%async_computation.7 | async-start | bytes 3244032 | tf_op jit(solution)/shard_map/reduce_scatter | solution.py:274
  (52 other events, 196.3 us)
Sparse Core Ops, SparseCore 0:
  10.9 57.8 all-gather.2
  526.2 147.6 reduce-scatter.9
  676.5 86.5 all-reduce.10
  765.8 135.1 reduce-scatter.7
  907.7 97.8 reduce-scatter.5
